TPU v7x, 32 devices: a whole 2x2x4 slice. The times are simulated.
32 devices in a mesh: heads: 8 (over y, x, core), batch: 4 (over z).
Axes of the slice: x: 2, y: 2, z: 4, core: 2. Of those that a mesh axis runs over, the one named last changes fastest.
Arguments:
- tokens: bfloat16 [2, 4, 1024, 2048], P(None, 'batch', 'heads'), may hold values from -6 to 6
- cotangent: bfloat16 [2, 4, 1024, 2048], P(None, 'batch', 'heads'), may hold values from -6 to 6
- doc_lengths: int32 [2, 4, 4], P(None, 'batch'), may hold values from 1 to 768, 1024 in all within a row
- pad_mask: int32 [2, 4, 1024], P(None, 'batch'), may hold values 0 or 1
- w_query: bfloat16 [2048, 1024], P(None, 'heads'), may hold values from -0.1875 to 0.1875
- w_key: bfloat16 [2048, 1024], P(None, 'heads'), may hold values from -0.1875 to 0.1875
- w_value: bfloat16 [2048, 1024], P(None, 'heads'), may hold values from -0.125 to 0.125
- w_out: bfloat16 [1024, 2048], P('heads'), may hold values from -0.75 to 0.75
- w_gate: bfloat16 [2048, 8192], P(None, 'heads'), may hold values from -0.125 to 0.125
- w_up: bfloat16 [2048, 8192], P(None, 'heads'), may hold values from -0.125 to 0.125
- w_down: bfloat16 [8192, 2048], P('heads'), may hold values from -0.0625 to 0.0625
- norm_attn: float32 [2048], replicated, may hold values from 0.1 to 1.9
- norm_mlp: float32 [2048], replicated, may hold values from 0.1 to 1.9
- mix_gate: float32 [8], P('heads'), may hold values from -2 to 2
Outputs:
- layer_out: bfloat16 [2, 4, 1024, 2048], P(None, 'batch', 'heads')
- grad_tokens: float32 [2, 4, 1024, 2048], P(None, 'batch', 'heads')
- grad_w_query: float32 [2048, 1024], P(None, 'heads')
- grad_w_key: float32 [2048, 1024], P(None, 'heads')
- grad_w_value: float32 [2048, 1024], P(None, 'heads')
- grad_w_out: float32 [1024, 2048], P('heads')
- grad_w_gate: float32 [2048, 8192], P(None, 'heads')
- grad_w_up: float32 [2048, 8192], P(None, 'heads')
- grad_w_down: float32 [8192, 2048], P('heads')
- grad_norm_attn: float32 [2048], replicated
- grad_norm_mlp: float32 [2048], replicated
- grad_mix_gate: float32 [8], P('heads')
Inputs may be any that keep to these rules, and one draw needn't show every extreme that they name: `doc_lengths`: the 4 lengths of a sequence sum to 1024; the longest is 768.
All inputs are finite; a program needn't handle non-finite values. No bound on the sum of `pad_mask` on one device may be relied on, other than what follows from the above.
Results may differ from a plain program's by a relative error of at most 0.018.
Values may be sent and summed in bfloat16 or wider, within the bound.
No kernel may reach another device: no remote copies, remote signals or barrier semaphores. Data moves between devices by JAX's collectives and lax.ppermute only.
A program may use at most 256 MiB of HBM per device.

v0:
```python
import jax
import jax.numpy as jnp
from jax import lax
from jax.sharding import PartitionSpec as P

DH = 128
SEG = 512
SEGS = 2
LEN = 1024
MICRO = 2
epsilon = 1e-05
big_negative = -1e30


def dot_rows(left_mat, right_mat):
    return lax.dot_general(
        left_mat, right_mat, (((1,), (1,)), ((), ())), preferred_element_type=jnp.float32
    )


def dot_cols(left_mat, right_mat):
    return lax.dot_general(
        left_mat, right_mat, (((0,), (0,)), ((), ())), preferred_element_type=jnp.float32
    )


def norm_rows(row_block, gain_vec):
    row_scale = lax.rsqrt(jnp.mean(row_block * row_block, axis=-1, keepdims=True) + epsilon)
    return (row_block * row_scale * gain_vec, row_scale)


def norm_back(row_block, row_scale, gain_vec, upstream):
    shaped = upstream * gain_vec
    inner = jnp.mean(shaped * row_block, axis=-1, keepdims=True)
    d_rows = row_scale * shaped - row_block * row_scale * row_scale * row_scale * inner
    d_gain = jnp.sum(upstream * row_block * row_scale, axis=0)
    return (d_rows, d_gain)


def positive(values_in):
    return jnp.where(values_in > 0, values_in + 1.0, jnp.exp(values_in))


def local_mask(begin_row, positions, doc_ids, valid_keys):
    seg_pos = positions[begin_row : begin_row + SEG]
    seg_doc = doc_ids[begin_row : begin_row + SEG]
    seg_valid = valid_keys[begin_row : begin_row + SEG]
    same_doc = seg_doc[:, None] == seg_doc[None, :]
    causal = seg_pos[None, :] <= seg_pos[:, None]
    return same_doc & causal & (seg_valid[None, :] | (seg_pos[None, :] == seg_pos[:, None]))


def memory_mask(begin_row, doc_ids, valid_keys):
    seg_doc = doc_ids[begin_row : begin_row + SEG]
    return (seg_doc[:, None] == doc_ids[None, :begin_row]) & valid_keys[None, :begin_row]


def head_forward(query_all, key_all, value_all, share, positions, doc_ids, valid_keys):
    score_scale = DH ** (-0.5)
    pos_query = positive(query_all.astype(jnp.float32)).astype(jnp.bfloat16)
    pos_key = positive(key_all.astype(jnp.float32)).astype(jnp.bfloat16)
    dotted_parts, recalled_parts, total_parts = ([], [], [])
    for segment in range(SEGS):
        begin_row = segment * SEG
        query_seg = query_all[begin_row : begin_row + SEG]
        key_seg = key_all[begin_row : begin_row + SEG]
        value_seg = value_all[begin_row : begin_row + SEG]
        allowed = local_mask(begin_row, positions, doc_ids, valid_keys)
        scores = jnp.where(allowed, dot_rows(query_seg, key_seg) * score_scale, big_negative)
        row_top = jnp.max(scores, axis=1, keepdims=True)
        log_total = row_top + jnp.log(jnp.sum(jnp.exp(scores - row_top), axis=1, keepdims=True))
        soft_probs = jnp.exp(scores - log_total)
        dotted_parts.append(
            jnp.dot(soft_probs.astype(jnp.bfloat16), value_seg, preferred_element_type=jnp.float32)
        )
        total_parts.append(log_total)
        if segment == 0:
            recalled_parts.append(jnp.zeros((SEG, DH), jnp.float32))
        else:
            mem_allowed = memory_mask(begin_row, doc_ids, valid_keys)
            weights = jnp.where(
                mem_allowed,
                dot_rows(pos_query[begin_row : begin_row + SEG], pos_key[:begin_row]),
                0.0,
            )
            denominator = jnp.maximum(jnp.sum(weights, axis=1, keepdims=True), 1.0)
            numerator = jnp.dot(
                weights.astype(jnp.bfloat16),
                value_all[:begin_row],
                preferred_element_type=jnp.float32,
            )
            recalled_parts.append(numerator / denominator)
    dotted = jnp.concatenate(dotted_parts, axis=0)
    recalled = jnp.concatenate(recalled_parts, axis=0)
    mixed_head = share * recalled + (1.0 - share) * dotted
    return (mixed_head, dotted, recalled, jnp.concatenate(total_parts, axis=0))


def head_backward(
    query_all,
    key_all,
    value_all,
    share,
    positions,
    doc_ids,
    valid_keys,
    d_mixed,
    dotted,
    recalled,
    log_totals,
):
    score_scale = DH ** (-0.5)
    query_float = query_all.astype(jnp.float32)
    key_float = key_all.astype(jnp.float32)
    pos_query = positive(query_float).astype(jnp.bfloat16)
    pos_key = positive(key_float).astype(jnp.bfloat16)
    d_share = jnp.sum(d_mixed * (recalled - dotted)) * share * (1.0 - share)
    d_dotted = ((1.0 - share) * d_mixed).astype(jnp.bfloat16)
    d_recalled = share * d_mixed
    zeros_block = jnp.zeros((LEN, DH), jnp.float32)
    d_query, d_key, d_value, d_posq, d_posk = (
        zeros_block,
        zeros_block,
        zeros_block,
        zeros_block,
        zeros_block,
    )
    for segment in range(SEGS):
        begin_row = segment * SEG
        end_row = begin_row + SEG
        query_seg = query_all[begin_row:end_row]
        key_seg = key_all[begin_row:end_row]
        value_seg = value_all[begin_row:end_row]
        allowed = local_mask(begin_row, positions, doc_ids, valid_keys)
        scores = jnp.where(allowed, dot_rows(query_seg, key_seg) * score_scale, big_negative)
        soft_probs = jnp.exp(scores - log_totals[begin_row:end_row])
        d_dot_seg = d_dotted[begin_row:end_row]
        d_value = d_value.at[begin_row:end_row].add(
            dot_cols(soft_probs.astype(jnp.bfloat16), d_dot_seg)
        )
        d_probs = dot_rows(d_dot_seg, value_seg)
        d_scores = (
            soft_probs * (d_probs - jnp.sum(soft_probs * d_probs, axis=1, keepdims=True))
        ).astype(jnp.bfloat16)
        d_query = d_query.at[begin_row:end_row].add(
            jnp.dot(d_scores, key_seg, preferred_element_type=jnp.float32) * score_scale
        )
        d_key = d_key.at[begin_row:end_row].add(dot_cols(d_scores, query_seg) * score_scale)
        if segment > 0:
            posq_seg = pos_query[begin_row:end_row]
            posk_prev = pos_key[:begin_row]
            value_prev = value_all[:begin_row]
            mem_allowed = memory_mask(begin_row, doc_ids, valid_keys)
            weights = jnp.where(mem_allowed, dot_rows(posq_seg, posk_prev), 0.0)
            row_total = jnp.sum(weights, axis=1, keepdims=True)
            denominator = jnp.maximum(row_total, 1.0)
            weights_low = weights.astype(jnp.bfloat16)
            numerator = jnp.dot(weights_low, value_prev, preferred_element_type=jnp.float32)
            d_recall_seg = d_recalled[begin_row:end_row]
            d_numer = (d_recall_seg / denominator).astype(jnp.bfloat16)
            d_denom = jnp.where(
                row_total > 1.0,
                -jnp.sum(d_recall_seg * numerator, axis=1, keepdims=True)
                / (denominator * denominator),
                0.0,
            )
            d_weights = jnp.where(mem_allowed, dot_rows(d_numer, value_prev) + d_denom, 0.0).astype(
                jnp.bfloat16
            )
            d_posq = d_posq.at[begin_row:end_row].add(
                jnp.dot(d_weights, posk_prev, preferred_element_type=jnp.float32)
            )
            d_posk = d_posk.at[:begin_row].add(dot_cols(d_weights, posq_seg))
            d_value = d_value.at[:begin_row].add(dot_cols(weights_low, d_numer))
    d_query = d_query + d_posq * jnp.where(query_float > 0, 1.0, jnp.exp(query_float))
    d_key = d_key + d_posk * jnp.where(key_float > 0, 1.0, jnp.exp(key_float))
    return (
        d_query.astype(jnp.bfloat16),
        d_key.astype(jnp.bfloat16),
        d_value.astype(jnp.bfloat16),
        d_share,
    )


def per_device(
    tokens,
    cotangent,
    doc_lengths,
    pad_mask,
    w_query,
    w_key,
    w_value,
    w_out,
    w_gate,
    w_up,
    w_down,
    norm_attn,
    norm_mlp,
    mix_gate,
):
    local_width = w_query.shape[1]
    hidden_cols = w_gate.shape[1]
    w_qkv = jnp.concatenate([w_query, w_key, w_value], axis=1)
    w_gate_up = jnp.concatenate([w_gate, w_up], axis=1)
    shares = jax.nn.sigmoid(mix_gate)
    positions = jnp.arange(LEN, dtype=jnp.int32)
    grad_qkv = jnp.zeros(w_qkv.shape, jnp.float32)
    grad_out = jnp.zeros(w_out.shape, jnp.float32)
    grad_gate_up = jnp.zeros(w_gate_up.shape, jnp.float32)
    grad_down = jnp.zeros(w_down.shape, jnp.float32)
    grad_mix = jnp.zeros(mix_gate.shape, jnp.float32)
    grad_gain_attn = jnp.zeros(norm_attn.shape, jnp.float32)
    grad_gain_mlp = jnp.zeros(norm_mlp.shape, jnp.float32)
    out_list, grad_in_list = ([], [])
    for micro_step in range(MICRO):
        doc_ends = jnp.cumsum(doc_lengths[micro_step, 0])
        doc_ids = jnp.sum((positions[:, None] >= doc_ends[None, :]).astype(jnp.int32), axis=1)
        valid_keys = pad_mask[micro_step, 0] == 1
        x_rows = tokens[micro_step, 0].astype(jnp.float32)
        normed_attn, scale_attn = norm_rows(x_rows, norm_attn)
        low_attn = normed_attn.astype(jnp.bfloat16)
        full_attn = lax.all_gather(low_attn, "heads", axis=0, tiled=True)
        qkv_all = jnp.dot(full_attn, w_qkv, preferred_element_type=jnp.float32).astype(jnp.bfloat16)
        head_inputs, head_kept, mixed_parts = ([], [], [])
        head_index = 0
        col_begin = head_index * DH
        query_all = qkv_all[:, col_begin : col_begin + DH]
        key_all = qkv_all[:, local_width + col_begin : local_width + col_begin + DH]
        value_all = qkv_all[:, 2 * local_width + col_begin : 2 * local_width + col_begin + DH]
        result_head = head_forward(
            query_all, key_all, value_all, shares[head_index], positions, doc_ids, valid_keys
        )
        head_inputs.append((query_all, key_all, value_all))
        head_kept.append(result_head)
        mixed_parts.append(result_head[0])
        mixed_low = mixed_parts[0].astype(jnp.bfloat16)
        attn_rows = lax.psum_scatter(
            jnp.dot(mixed_low, w_out, preferred_element_type=jnp.float32),
            "heads",
            scatter_dimension=0,
            tiled=True,
        )
        mid_rows = x_rows + attn_rows
        normed_mlp, scale_mlp = norm_rows(mid_rows, norm_mlp)
        low_mlp = normed_mlp.astype(jnp.bfloat16)
        full_mlp = lax.all_gather(low_mlp, "heads", axis=0, tiled=True)
        gate_up = jnp.dot(full_mlp, w_gate_up, preferred_element_type=jnp.float32)
        gate_pre = gate_up[:, :hidden_cols]
        up_pre = gate_up[:, hidden_cols:]
        sig_gate = jax.nn.sigmoid(gate_pre)
        hidden = (gate_pre * sig_gate * up_pre).astype(jnp.bfloat16)
        mlp_rows = lax.psum_scatter(
            jnp.dot(hidden, w_down, preferred_element_type=jnp.float32).astype(jnp.bfloat16),
            "heads",
            scatter_dimension=0,
            tiled=True,
        ).astype(jnp.float32)
        out_list.append((mid_rows + mlp_rows).astype(jnp.bfloat16))
        cot_low = cotangent[micro_step, 0]
        cot_full = lax.all_gather(cot_low, "heads", axis=0, tiled=True)
        grad_down = grad_down + dot_cols(hidden, cot_full)
        d_hidden = dot_rows(cot_full, w_down)
        d_up = d_hidden * gate_pre * sig_gate
        d_gate = d_hidden * up_pre * sig_gate * (1.0 + gate_pre * (1.0 - sig_gate))
        d_gate_up = jnp.concatenate([d_gate, d_up], axis=1).astype(jnp.bfloat16)
        grad_gate_up = grad_gate_up + dot_cols(full_mlp, d_gate_up)
        d_norm_mlp = lax.psum_scatter(
            dot_rows(d_gate_up, w_gate_up), "heads", scatter_dimension=0, tiled=True
        )
        d_mid_norm, gain_mlp_part = norm_back(mid_rows, scale_mlp, norm_mlp, d_norm_mlp)
        grad_gain_mlp = grad_gain_mlp + gain_mlp_part
        d_mid = d_mid_norm + cot_low.astype(jnp.float32)
        d_attn_full = lax.all_gather(d_mid.astype(jnp.bfloat16), "heads", axis=0, tiled=True)
        grad_out = grad_out + dot_cols(mixed_low, d_attn_full)
        d_mixed_all = dot_rows(d_attn_full, w_out)
        dq_parts, dk_parts, dv_parts, dshare_parts = ([], [], [], [])
        head_index = 0
        col_begin = head_index * DH
        query_all, key_all, value_all = head_inputs[head_index]
        kept_head = head_kept[head_index]
        back_head = head_backward(
            query_all,
            key_all,
            value_all,
            shares[head_index],
            positions,
            doc_ids,
            valid_keys,
            d_mixed_all,
            kept_head[1],
            kept_head[2],
            kept_head[3],
        )
        dq_parts.append(back_head[0])
        dk_parts.append(back_head[1])
        dv_parts.append(back_head[2])
        dshare_parts.append(back_head[3])
        grad_mix = grad_mix + jnp.stack(dshare_parts)
        d_qkv = jnp.concatenate(dq_parts + dk_parts + dv_parts, axis=1)
        grad_qkv = grad_qkv + dot_cols(full_attn, d_qkv)
        d_norm_attn = lax.psum_scatter(
            dot_rows(d_qkv, w_qkv).astype(jnp.bfloat16), "heads", scatter_dimension=0, tiled=True
        ).astype(jnp.float32)
        d_x_norm, gain_attn_part = norm_back(x_rows, scale_attn, norm_attn, d_norm_attn)
        grad_gain_attn = grad_gain_attn + gain_attn_part
        grad_in_list.append(d_x_norm + d_mid)
    grad_qkv, grad_out, grad_gate_up, grad_down, grad_mix = (
        lax.psum(grad_qkv.astype(jnp.bfloat16), "batch").astype(jnp.float32),
        lax.psum(grad_out.astype(jnp.bfloat16), "batch").astype(jnp.float32),
        lax.psum(grad_gate_up.astype(jnp.bfloat16), "batch").astype(jnp.float32),
        lax.psum(grad_down.astype(jnp.bfloat16), "batch").astype(jnp.float32),
        lax.psum(grad_mix.astype(jnp.bfloat16), "batch").astype(jnp.float32),
    )
    grad_gain_attn, grad_gain_mlp = lax.psum((grad_gain_attn, grad_gain_mlp), ("heads", "batch"))
    layer_out = jnp.stack(out_list)[:, None]
    grad_tokens = jnp.stack(grad_in_list)[:, None]
    return (
        layer_out,
        grad_tokens,
        grad_qkv[:, :local_width],
        grad_qkv[:, local_width : 2 * local_width],
        grad_qkv[:, 2 * local_width :],
        grad_out,
        grad_gate_up[:, :hidden_cols],
        grad_gate_up[:, hidden_cols:],
        grad_down,
        grad_gain_attn,
        grad_gain_mlp,
        grad_mix,
    )


def solution(mesh):
    in_specs = (
        P(None, "batch", "heads", None),
        P(None, "batch", "heads", None),
        P(None, "batch", None),
        P(None, "batch", None),
        P(None, "heads"),
        P(None, "heads"),
        P(None, "heads"),
        P("heads", None),
        P(None, "heads"),
        P(None, "heads"),
        P("heads", None),
        P(),
        P(),
        P("heads"),
    )
    out_specs = (
        P(None, "batch", "heads", None),
        P(None, "batch", "heads", None),
        P(None, "heads"),
        P(None, "heads"),
        P(None, "heads"),
        P("heads", None),
        P(None, "heads"),
        P(None, "heads"),
        P("heads", None),
        P(),
        P(),
        P("heads"),
    )
    return jax.shard_map(
        per_device, mesh=mesh, in_specs=in_specs, out_specs=out_specs, check_vma=False
    )
```

profile of v0, /device:TPU:0, one launch (start us, length us, event | category | flops | bytes accessed | tf_op | source)
XLA Modules:
  0.0 1430.8 jit_solution(2356076530199268857)
XLA Ops:
  9.5 2.5 fusion.36
  16.6 35.0 %all-gather.15.cloned.1.call-done = bf16[1024,2048]{1,0:T(8,128)(2,1)} async-done(((bf16[128,2048]{1,0:T(8,128)(2,1)}), bf16[1024,2048]{1,0:T(8,128)(2,1)}) %all-gather.15.cloned.1.call-update) | async-done | bytes 4194320 | tf_op jit(solution)/shard_map/all_gather | solution.py:222
  51.6 4.5 convolution_convert_fusion.4
  63.0 4.7 fusion.168
  68.3 22.5 %all-gather.11.cloned.1.call-done = bf16[1024,2048]{1,0:T(8,128)(2,1)} async-done(((bf16[128,2048]{1,0:T(8,128)(2,1)}), bf16[1024,2048]{1,0:T(8,128)(2,1)}) %all-gather.11.cloned.1.call-update) | async-done | bytes 4194320 | tf_op jit(solution)/shard_map/all_gather | solution.py:222
  90.8 4.5 convolution_convert_fusion.5
  102.3 5.7 fusion.166
  108.1 58.1 %reduce-scatter.13.cloned.1.call-done = f32[128,2048]{1,0:T(8,128)} async-done(((f32[1024,2048]{1,0:T(8,128)}), f32[128,2048]{1,0:T(8,128)}) %reduce-scatter.13.cloned.1.call-update) | async-done | bytes 1048592 | tf_op jit(solution)/shard_map/reduce_scatter | solution.py:237
  166.2 75.6 %reduce-scatter.9.cloned.1.call-done = f32[128,2048]{1,0:T(8,128)} async-done(((f32[1024,2048]{1,0:T(8,128)}), f32[128,2048]{1,0:T(8,128)}) %reduce-scatter.9.cloned.1.call-update) | async-done | bytes 1048592 | tf_op jit(solution)/shard_map/reduce_scatter | solution.py:237
  241.8 2.8 multiply_reduce_fusion.9
  248.0 4.8 constant_dynamic-update-slice_fusion.4
  252.8 2.5 constant_dynamic-update-slice_fusion.3
  255.3 27.2 %all-gather.13.cloned.1.call-done = bf16[1024,2048]{1,0:T(8,128)(2,1)} async-done(((bf16[128,2048]{1,0:T(8,128)(2,1)}), bf16[1024,2048]{1,0:T(8,128)(2,1)}) %all-gather.13.cloned.1.call-update) | async-done | bytes 4194320 | tf_op jit(solution)/shard_map/all_gather | solution.py:246
  282.4 14.9 %fusion.167 = f32[1024,2048]{1,0:T(8,128)} fusion(bf16[1024,2048]{1,0:T(8,128)(2,1)} %all-gather.13.cloned.1.call-done, bf16[2048,2048]{1,0:T(8,128)(2,1)} %constant_dynamic-update-slice_fusion.3), kind=kOutput, calls=%fused_computation.320 | convolution fusion | flops 8589934592 | bytes 20971520 | tf_op jit(solution)/shard_map/dot_general | solution.py:247
  297.3 24.2 %all-gather.23.cloned.1.call-done = bf16[1,1,1024,2048]{3,2,1,0:T(8,128)(2,1)} async-done(((bf16[1,1,128,2048]{3,2,1,0:T(8,128)(2,1)}), bf16[1,1,1024,2048]{3,2,1,0:T(8,128)(2,1)}) %all-gather.23.cloned.1.call-update) | async-done | bytes 4194320 | tf_op jit(solution)/shard_map/all_gather | solution.py:260
  321.5 13.2 multiply_convert_fusion.3
  336.7 13.3 fusion.12
  350.1 71.3 %reduce-scatter.17.cloned.1.call-done = f32[128,2048]{1,0:T(8,128)} async-done(((f32[1024,2048]{1,0:T(8,128)}), f32[128,2048]{1,0:T(8,128)}) %reduce-scatter.17.cloned.1.call-update) | async-done | bytes 1048592 | tf_op jit(solution)/shard_map/reduce_scatter | solution.py:267
  421.5 3.0 multiply_reduce_fusion.1
  425.2 36.1 %all-gather.17.cloned.1.call-done = bf16[1024,2048]{1,0:T(8,128)(2,1)} async-done(((bf16[128,2048]{1,0:T(8,128)(2,1)}), bf16[1024,2048]{1,0:T(8,128)(2,1)}) %all-gather.17.cloned.1.call-update) | async-done | bytes 4194320 | tf_op jit(solution)/shard_map/all_gather | solution.py:246
  461.3 14.6 %fusion.169 = f32[1024,2048]{1,0:T(8,128)} fusion(bf16[1024,2048]{1,0:T(8,128)(2,1)} %all-gather.17.cloned.1.call-done, bf16[2048,2048]{1,0:T(8,128)(2,1)} %constant_dynamic-update-slice_fusion.3), kind=kOutput, calls=%fused_computation.322 | convolution fusion | flops 8589934592 | bytes 20971520 | tf_op jit(solution)/shard_map/dot_general | solution.py:247
  475.9 24.7 %all-gather.25.cloned.1.call-done = bf16[1,1,1024,2048]{3,2,1,0:T(8,128)(2,1)} async-done(((bf16[1,1,128,2048]{3,2,1,0:T(8,128)(2,1)}), bf16[1,1,1024,2048]{3,2,1,0:T(8,128)(2,1)}) %all-gather.25.cloned.1.call-update) | async-done | bytes 4194320 | tf_op jit(solution)/shard_map/all_gather | solution.py:260
  500.7 13.2 multiply_convert_fusion.1
  516.0 13.3 fusion.10
  529.8 9.7 convolution_convert_fusion.3
  539.6 10.4 convolution_convert_fusion.2
  550.1 50.7 %reduce-scatter.21.cloned.1.call-done = f32[128,2048]{1,0:T(8,128)} async-done(((f32[1024,2048]{1,0:T(8,128)}), f32[128,2048]{1,0:T(8,128)}) %reduce-scatter.21.cloned.1.call-update) | async-done | bytes 1048592 | tf_op jit(solution)/shard_map/reduce_scatter | solution.py:267
  602.3 53.8 %reduce-scatter.11.cloned.1.call-done = bf16[128,2048]{1,0:T(8,128)(2,1)} async-done(((bf16[1024,2048]{1,0:T(8,128)(2,1)}), bf16[128,2048]{1,0:T(8,128)(2,1)}) %reduce-scatter.11.cloned.1.call-update) | async-done | bytes 524304 | tf_op jit(solution)/shard_map/reduce_scatter | solution.py:252
  656.1 55.5 %reduce-scatter.15.cloned.1.call-done = bf16[128,2048]{1,0:T(8,128)(2,1)} async-done(((bf16[1024,2048]{1,0:T(8,128)(2,1)}), bf16[128,2048]{1,0:T(8,128)(2,1)}) %reduce-scatter.15.cloned.1.call-update) | async-done | bytes 524304 | tf_op jit(solution)/shard_map/reduce_scatter | solution.py:252
  711.5 4.5 fusion.153
  716.8 36.1 %all-gather.21.cloned.1.call-done = bf16[1024,2048]{1,0:T(8,128)(2,1)} async-done(((bf16[128,2048]{1,0:T(8,128)(2,1)}), bf16[1024,2048]{1,0:T(8,128)(2,1)}) %all-gather.21.cloned.1.call-update) | async-done | bytes 4194320 | tf_op jit(solution)/shard_map/all_gather | solution.py:273
  753.0 4.6 fusion.65
  763.2 5.9 convolution_convert_fusion
  770.8 14.8 %fusion.11 = f32[2048,2048]{1,0:T(8,128)} fusion(bf16[1024,2048]{1,0:T(8,128)(2,1)} %all-gather.13.cloned.1.call-done, bf16[1024,1024]{1,0:T(8,128)(2,1)} %copy-done.110, bf16[1024,1024]{1,0:T(8,128)(2,1)S(1)} %copy-done.109), kind=kOutput, calls=%fused_computation.26 | convolution fusion | flops 8598323200 | bytes 25165824 | tf_op jit(solution)/shard_map/dot_general | solution.py:22
  785.6 6.4 all-gather.19.cloned.1.call-done
  792.0 4.6 fusion.61
  802.3 6.0 convolution_convert_fusion.1
  808.7 7.3 fusion
  816.0 6.2 add_convert_fusion.1
  822.2 16.9 %add_convert_fusion = bf16[2048,2048]{1,0:T(8,128)(2,1)} fusion(f32[2048,2048]{1,0:T(8,128)} %fusion.11, bf16[1024,2048]{1,0:T(8,128)(2,1)} %all-gather.17.cloned.1.call-done, bf16[1024,1024]{1,0:T(8,128)(2,1)} %copy-done.112, bf16[1024,1024]{1,0:T(8,128)(2,1)} %copy-done.111), kind=kOutput, calls=%fused_computation | convolution fusion | flops 8606711808 | bytes 33554432 | tf_op jit(solution)/shard_map/dot_general | solution.py:22
  843.9 2.4 fusion.72
  846.3 3.6 add_convert_fusion.2
  854.4 12.8 psum.55
  867.9 34.8 %reduce-scatter.19.cloned.1.call-done = bf16[128,2048]{1,0:T(8,128)(2,1)} async-done(((bf16[1024,2048]{1,0:T(8,128)(2,1)}), bf16[128,2048]{1,0:T(8,128)(2,1)}) %reduce-scatter.19.cloned.1.call-update) | async-done | bytes 524304 | tf_op jit(solution)/shard_map/reduce_scatter | solution.py:301
  904.6 45.3 %all-reduce.6 = (f32[2048]{0:T(1024)}, f32[2048]{0:T(1024)}) all-reduce(f32[2048]{0:T(1024)S(1)} %add.352, f32[2048]{0:T(1024)S(1)} %add.353), channel_id=1, replica_groups=mesh['heads'=8,'batch'=4] {'heads','batch'}, use_global_device_ids=true, to_apply=%region_42.43 | all-reduce | flops 4096 | bytes 32768 | tf_op jit(solution)/shard_map/psum | solution.py:314
  953.6 449.8 %all-reduce.10.cloned.1.call-done = (bf16[2048,384]{1,0:T(8,128)(2,1)}, bf16[2048,2048]{1,0:T(8,128)(2,1)}, bf16[128,2048]{1,0:T(8,128)(2,1)}, bf16[1024,2048]{1,0:T(8,128)(2,1)}) async-done(((bf16[2048,384]{1,0:T(8,128)(2,1)}, bf16[2048,2048]{1,0:T(8,128)(2,1)}, bf16[128,2048]{1,0:T(8,128)(2,1)}, bf16[1024,2048]{1,0:T(8,128)(2,1)}), (bf16[2048,384]{1,0:T(8,128)(2,1)}, bf16[2048,2048]{1,0:T(8,128)(2,1)}, ...) | async-done | bytes 14680080 | tf_op jit(solution)/shard_map/psum | solution.py:308
  1403.4 11.9 fusion.155
  1415.3 4.4 convert_element_type.296
  (367 shorter events, 60.1 us)
Async XLA Ops:
  7.2 55.9 %copy-start = (bf16[128,2048]{1,0:T(8,128)(2,1)S(1)}, bf16[128,2048]{1,0:T(8,128)(2,1)}, u32[]{:S(2)}) copy-start(bf16[128,2048]{1,0:T(8,128)(2,1)} %param.57) | copy-start | bytes 1572868
  7.2 44.3 %all-gather.15.cloned.1.call-start = ((), (), s32[]{:S(2)}) async-start(), calls=%async_computation.12 | async-start | bytes 4718592 | tf_op jit(solution)/shard_map/all_gather | solution.py:222
  12.0 78.8 %all-gather.11.cloned.1.call-start = ((), (), s32[]{:S(2)}) async-start(), calls=%async_computation.8 | async-start | bytes 4718592 | tf_op jit(solution)/shard_map/all_gather | solution.py:222
  12.8 153.4 %reduce-scatter.13.cloned.1.call-start = ((), (), s32[]{:S(2)}) async-start(), calls=%async_computation.13 | async-start | bytes 9437184 | tf_op jit(solution)/shard_map/reduce_scatter | solution.py:237
  13.8 44.4 %copy-start.98 = (pred[512]{0:T(512)(128)(4,1)}, pred[512]{0:T(512)(128)(4,1)S(1)}, u32[]{:S(2)}) copy-start(pred[512]{0:T(512)(128)(4,1)S(1)} %get-tuple-element.267) | copy-start | bytes 1540
  14.0 44.3 %copy-start.91 = (s32[512]{0:T(512)}, s32[512]{0:T(512)S(1)}, u32[]{:S(2)}) copy-start(s32[512]{0:T(512)S(1)} %get-tuple-element.330) | copy-start | bytes 6148
  14.0 44.3 %copy-start.93 = (s32[512]{0:T(512)}, s32[512]{0:T(512)S(1)}, u32[]{:S(2)}) copy-start(s32[512]{0:T(512)S(1)} %get-tuple-element.331) | copy-start | bytes 6148
  67.7 174.1 %reduce-scatter.9.cloned.1.call-start = ((), (), s32[]{:S(2)}) async-start(), calls=%async_computation.9 | async-start | bytes 9437184 | tf_op jit(solution)/shard_map/reduce_scatter | solution.py:237
  68.2 29.3 %copy-start.96 = (pred[512]{0:T(512)(128)(4,1)}, pred[512]{0:T(512)(128)(4,1)S(1)}, u32[]{:S(2)}) copy-start(pred[512]{0:T(512)(128)(4,1)S(1)} %get-tuple-element.265) | copy-start | bytes 1540
  68.3 29.2 %copy-start.87 = (s32[512]{0:T(512)}, s32[512]{0:T(512)S(1)}, u32[]{:S(2)}) copy-start(s32[512]{0:T(512)S(1)} %get-tuple-element.328) | copy-start | bytes 6148
  68.3 29.2 %copy-start.89 = (s32[512]{0:T(512)}, s32[512]{0:T(512)S(1)}, u32[]{:S(2)}) copy-start(s32[512]{0:T(512)S(1)} %get-tuple-element.329) | copy-start | bytes 6148
  108.0 133.8 %copy-start.9 = (bf16[2,1,128,2048]{3,2,1,0:T(8,128)(2,1)S(1)}, bf16[2,1,128,2048]{3,2,1,0:T(8,128)(2,1)}, u32[]{:S(2)}) copy-start(bf16[2,1,128,2048]{3,2,1,0:T(8,128)(2,1)} %param.50) | copy-start | bytes 3145732
  108.0 136.6 %copy-start.63 = (f32[2048]{0:T(1024)S(1)}, f32[2048]{0:T(1024)}, u32[]{:S(2)}) copy-start(f32[2048]{0:T(1024)} %param.62) | copy-start | bytes 24580
  108.0 174.4 %all-gather.13.cloned.1.call-start = ((), (), s32[]{:S(2)}) async-start(), calls=%async_computation.10 | async-start | bytes 4718592 | tf_op jit(solution)/shard_map/all_gather | solution.py:246
  245.6 75.9 %all-gather.23.cloned.1.call-start = ((), (), s32[]{:S(2)}) async-start(), calls=%async_computation.22 | async-start | bytes 4718592 | tf_op jit(solution)/shard_map/all_gather | solution.py:260
  247.9 173.5 %reduce-scatter.17.cloned.1.call-start = ((), (), s32[]{:S(2)}) async-start(), calls=%async_computation.16 | async-start | bytes 9437184 | tf_op jit(solution)/shard_map/reduce_scatter | solution.py:267
  350.0 71.4 %copy-start.11 = (f32[128,2048]{1,0:T(8,128)S(1)}, f32[128,2048]{1,0:T(8,128)}, u32[]{:S(2)}) copy-start(f32[128,2048]{1,0:T(8,128)} %get-tuple-element.304) | copy-start | bytes 3145732
  350.0 111.3 %all-gather.17.cloned.1.call-start = ((), (), s32[]{:S(2)}) async-start(), calls=%async_computation.14 | async-start | bytes 4718592 | tf_op jit(solution)/shard_map/all_gather | solution.py:246
  424.5 76.2 %all-gather.25.cloned.1.call-start = ((), (), s32[]{:S(2)}) async-start(), calls=%async_computation.23 | async-start | bytes 4718592 | tf_op jit(solution)/shard_map/all_gather | solution.py:260
  425.2 175.6 %reduce-scatter.21.cloned.1.call-start = ((), (), s32[]{:S(2)}) async-start(), calls=%async_computation.19 | async-start | bytes 9437184 | tf_op jit(solution)/shard_map/reduce_scatter | solution.py:267
  529.3 126.7 %reduce-scatter.11.cloned.1.call-start = ((), (), s32[]{:S(2)}) async-start(), calls=%async_computation.11 | async-start | bytes 4718592 | tf_op jit(solution)/shard_map/reduce_scatter | solution.py:252
  539.5 172.0 %reduce-scatter.15.cloned.1.call-start = ((), (), s32[]{:S(2)}) async-start(), calls=%async_computation.15 | async-start | bytes 4718592 | tf_op jit(solution)/shard_map/reduce_scatter | solution.py:252
  550.0 202.9 %all-gather.21.cloned.1.call-start = ((), (), s32[]{:S(2)}) async-start(), calls=%async_computation.20 | async-start | bytes 4718592 | tf_op jit(solution)/shard_map/all_gather | solution.py:273
  716.1 41.5 %copy-start.6 = (f32[512,512]{0,1:T(8,128)S(1)}, f32[512,512]{0,1:T(8,128)}, u32[]{:S(2)}) copy-start(f32[512,512]{0,1:T(8,128)} %copy-done.5) | copy-start | bytes 3145732
  716.1 41.4 %copy-start.70 = (f32[512]{0:T(512)S(1)}, f32[512]{0:T(512)}, u32[]{:S(2)}) copy-start(f32[512]{0:T(512)} %copy-done.69) | copy-start | bytes 6148
  716.1 75.9 %all-gather.19.cloned.1.call-start = ((), (), s32[]{:S(2)}) async-start(), calls=%async_computation.17 | async-start | bytes 4718592 | tf_op jit(solution)/shard_map/all_gather | solution.py:273
  716.7 41.2 %copy-start.8 = (f32[512,512]{0,1:T(8,128)S(1)}, f32[512,512]{0,1:T(8,128)}, u32[]{:S(2)}) copy-start(f32[512,512]{0,1:T(8,128)} %copy-done.7) | copy-start | bytes 3145732
  716.7 41.2 %copy-start.72 = (f32[512]{0:T(512)S(1)}, f32[512]{0:T(512)}, u32[]{:S(2)}) copy-start(f32[512]{0:T(512)} %copy-done.71) | copy-start | bytes 6148
  716.7 41.6 %copy-start.77 = (f32[512]{0:T(512)S(1)}, f32[512]{0:T(512)}, u32[]{:S(2)}) copy-start(f32[512]{0:T(512)} %copy-done.76) | copy-start | bytes 6148
  716.7 41.6 %copy-start.15 = (bf16[1024,384]{0,1:T(8,128)(2,1)S(1)}, bf16[1024,384]{0,1:T(8,128)(2,1)}, u32[]{:S(2)}) copy-start(bf16[1024,384]{0,1:T(8,128)(2,1)} %copy-done.14) | copy-start | bytes 2359300
  716.7 41.6 %copy-start.86 = (f32[512]{0:T(512)S(1)}, f32[512]{0:T(512)}, u32[]{:S(2)}) copy-start(f32[512]{0:T(512)} %copy-done.85) | copy-start | bytes 6148
  716.8 41.6 %copy-start.92 = (s32[512]{0:T(512)S(1)}, s32[512]{0:T(512)}, u32[]{:S(2)}) copy-start(s32[512]{0:T(512)} %copy-done.91) | copy-start | bytes 6148
  716.8 41.6 %copy-start.94 = (s32[512]{0:T(512)S(1)}, s32[512]{0:T(512)}, u32[]{:S(2)}) copy-start(s32[512]{0:T(512)} %copy-done.93) | copy-start | bytes 6148
  716.8 41.6 %copy-start.99 = (pred[512]{0:T(512)(128)(4,1)S(1)}, pred[512]{0:T(512)(128)(4,1)}, u32[]{:S(2)}) copy-start(pred[512]{0:T(512)(128)(4,1)} %copy-done.98) | copy-start | bytes 1540
  716.8 151.1 %reduce-scatter.23.cloned.1.call-start = ((), (), s32[]{:S(2)}) async-start(), calls=%async_computation.21 | async-start | bytes 4718592 | tf_op jit(solution)/shard_map/reduce_scatter | solution.py:301
  769.2 133.5 %reduce-scatter.19.cloned.1.call-start = ((), (), s32[]{:S(2)}) async-start(), calls=%async_computation.18 | async-start | bytes 4718592 | tf_op jit(solution)/shard_map/reduce_scatter | solution.py:301
  785.6 11.9 copy-start.13
  785.6 11.9 copy-start.84
  785.6 11.9 copy-start.88
  808.4 595.0 %all-reduce.10.cloned.1.call-start = ((), (), s32[]{:S(2)}) async-start(), calls=%async_computation.24 | async-start | bytes 29360128 | tf_op jit(solution)/shard_map/psum | solution.py:308
  822.2 16.9 %copy-start.20 = (bf16[1024,2048]{1,0:T(8,128)(2,1)S(1)}, bf16[1024,2048]{1,0:T(8,128)(2,1)}, u32[]{:S(2)}) copy-start(bf16[1024,2048]{1,0:T(8,128)(2,1)} %all-gather.19.cloned.1.call-done) | copy-start | bytes 12582916
  822.2 16.9 %copy-start.25 = (bf16[1024,128]{0,1:T(8,128)(2,1)S(1)}, bf16[1024,128]{0,1:T(8,128)(2,1)}, u32[]{:S(2)}) copy-start(bf16[1024,128]{0,1:T(8,128)(2,1)} %copy-done.24) | copy-start | bytes 786436
  850.0 52.8 %copy-start.10 = (bf16[2,1,128,2048]{3,2,1,0:T(8,128)(2,1)S(1)}, bf16[2,1,128,2048]{3,2,1,0:T(8,128)(2,1)}, u32[]{:S(2)}) copy-start(bf16[2,1,128,2048]{3,2,1,0:T(8,128)(2,1)} %param.50) | copy-start | bytes 3145732
  850.0 52.8 %copy-start.64 = (f32[2048]{0:T(1024)S(1)}, f32[2048]{0:T(1024)}, u32[]{:S(2)}) copy-start(f32[2048]{0:T(1024)} %param.61) | copy-start | bytes 24580
  850.0 52.8 %copy-start.80 = (f32[128]{0:T(128)S(1)}, f32[128]{0:T(128)}, u32[]{:S(2)}) copy-start(f32[128]{0:T(128)} %copy-done.79) | copy-start | bytes 1540
  850.0 52.7 %copy-start.82 = (f32[128]{0:T(128)S(1)}, f32[128]{0:T(128)}, u32[]{:S(2)}) copy-start(f32[128]{0:T(128)} %copy-done.81) | copy-start | bytes 1540
  850.0 99.9 %copy-start.21 = (f32[128,2048]{1,0:T(8,128)S(1)}, f32[128,2048]{1,0:T(8,128)}, u32[]{:S(2)}) copy-start(f32[128,2048]{1,0:T(8,128)} %get-tuple-element.275) | copy-start | bytes 3145732
  1403.4 11.9 copy-start.17
  (82 other events, 281.4 us)
Sparse Core Ops, SparseCore 0:
  12.1 39.4 all-gather.14
  54.1 36.7 all-gather.10
  94.8 71.3 reduce-scatter.12
  170.5 71.2 reduce-scatter.8
  245.7 36.6 all-gather.12
  284.8 36.7 all-gather.22
  350.2 71.2 reduce-scatter.16
  424.6 36.6 all-gather.16
  463.9 36.7 all-gather.24
  529.4 71.2 reduce-scatter.20
  604.7 51.3 reduce-scatter.10
  660.2 51.2 reduce-scatter.14
  716.2 36.6 all-gather.20
  755.3 36.7 all-gather.18
  795.8 51.3 reduce-scatter.22
  851.3 51.3 reduce-scatter.18
  906.6 496.7 all-reduce.9
where the time goes:
time: 1440 us; the launch traced here: 1430 us
  waiting for transfers between devices  1060 us (74%)
  matrix products  211 us (15%)
  blocking collectives  58.1 us (4%)
  local copies, waits for them, and re-layouts  42.1 us (3%)
  other arithmetic  34.4 us (2%)
  between operations  19.9 us (1%)
    psum x1, waiting for transfers between devices, per_device(): lax.psum(grad_qkv.astype(jnp.bfloat16), 'batch').astype(jnp.float32)  450 us
    reduce_scatter x2, waiting for transfers between devices, per_device(): lax.psum_scatter(jnp.dot(mixed_low, w_out, preferred_element_type=jnp.flo...  134 us
    reduce_scatter x2, waiting for transfers between devices, per_device(): lax.psum_scatter(dot_rows(d_gate_up, w_gate_up), 'heads', scatter_dimensi...  122 us
    reduce_scatter x2, waiting for transfers between devices, per_device(): lax.psum_scatter(jnp.dot(hidden, w_down, preferred_element_type=jnp.float...  109 us
    dot_general x20, matrix products, dot_rows(): lax.dot_general(left_mat, right_mat, (((1,), (1,)), ((), ())), preferred_...  79.7 us
    all_gather x2, waiting for transfers between devices, per_device(): full_mlp = lax.all_gather(low_mlp, 'heads', axis=0, tiled=True)  63.2 us
    all_gather x2, waiting for transfers between devices, per_device(): full_attn = lax.all_gather(low_attn, 'heads', axis=0, tiled=True)  57.5 us
    dot_general x20, matrix products, dot_cols(): lax.dot_general(left_mat, right_mat, (((0,), (0,)), ((), ())), preferred_...  57.2 us
  transfers between devices with their start and end apart: 17, of which 16 were waited for; matrix products, arithmetic and copies ran while one was open for 13% of the time, Pallas kernels for 0%

commit v1 on v0

--- a/solution.py
+++ b/solution.py
@@ -2,6 +2,7 @@
 import jax.numpy as jnp
 from jax import lax
 from jax.sharding import PartitionSpec as P
+from jax.lax import all_gather
 
 DH = 128
 SEG = 512
@@ -10,6 +11,10 @@
 MICRO = 2
 epsilon = 1e-05
 big_negative = -1e30
+
+
+def draw_wall_over_axis(array_here):
+    return jnp.sum(all_gather(array_here, axis_name="batch"), axis=0)
 
 
 def dot_rows(left_mat, right_mat):
@@ -305,7 +310,7 @@
         grad_gain_attn = grad_gain_attn + gain_attn_part
         grad_in_list.append(d_x_norm + d_mid)
     grad_qkv, grad_out, grad_gate_up, grad_down, grad_mix = (
-        lax.psum(grad_qkv.astype(jnp.bfloat16), "batch").astype(jnp.float32),
+        draw_wall_over_axis(grad_qkv.astype(jnp.bfloat16)).astype(jnp.float32),
         lax.psum(grad_out.astype(jnp.bfloat16), "batch").astype(jnp.float32),
         lax.psum(grad_gate_up.astype(jnp.bfloat16), "batch").astype(jnp.float32),
         lax.psum(grad_down.astype(jnp.bfloat16), "batch").astype(jnp.float32),

time: 1440 us -> 1500 us (1.042)
  waiting for transfers between devices: 1060 us -> 1120 us
    all_gather x0 -> x1, waiting for transfers between devices: none -> 63.6 us  [draw_wall_over_axis(): return jnp.sum(all_gather(array_here, axis_name='batch'), axis=0)]
    all_gather x2, waiting for transfers between devices: 42.5 us -> 58.6 us  [per_device(): lax.all_gather(d_mid.astype(jnp.bfloat16), 'heads', axis=0, tiled=True)]
    reduce_scatter x2, waiting for transfers between devices: 34.8 us -> 18.9 us  [per_device(): lax.psum_scatter(dot_rows(d_qkv, w_qkv).astype(jnp.bfloat16), 'heads', sc...]
  transfers between devices with their start and end apart: 17 -> 18, of which waited for: 16 -> 17; matrix products, arithmetic and copies ran while one was open for 13% -> 13% of each run, Pallas kernels for 0% -> 0%
where the time goes in v1:
time: 1500 us; the launch traced here: 1490 us
  waiting for transfers between devices  1120 us (75%)
  matrix products  211 us (14%)
  blocking collectives  61.6 us (4%)
  local copies, waits for them, and re-layouts  41.1 us (3%)
  other arithmetic  39.2 us (3%)
  between operations  20 us (1%)
    psum x1, waiting for transfers between devices, per_device(): lax.psum(grad_gate_up.astype(jnp.bfloat16), 'batch').astype(jnp.float32)  439 us
    reduce_scatter x2, waiting for transfers between devices, per_device(): lax.psum_scatter(jnp.dot(mixed_low, w_out, preferred_element_type=jnp.flo...  134 us
    reduce_scatter x2, waiting for transfers between devices, per_device(): lax.psum_scatter(dot_rows(d_gate_up, w_gate_up), 'heads', scatter_dimensi...  122 us
    reduce_scatter x2, waiting for transfers between devices, per_device(): lax.psum_scatter(jnp.dot(hidden, w_down, preferred_element_type=jnp.float...  109 us
    dot_general x20, matrix products, dot_rows(): lax.dot_general(left_mat, right_mat, (((1,), (1,)), ((), ())), preferred_...  79.7 us
    all_gather x1, waiting for transfers between devices, draw_wall_over_axis(): return jnp.sum(all_gather(array_here, axis_name='batch'), axis=0)  63.6 us
    all_gather x2, waiting for transfers between devices, per_device(): full_mlp = lax.all_gather(low_mlp, 'heads', axis=0, tiled=True)  63.2 us
    all_gather x2, waiting for transfers between devices, per_device(): lax.all_gather(d_mid.astype(jnp.bfloat16), 'heads', axis=0, tiled=True)  58.6 us
  transfers between devices with their start and end apart: 18, of which 17 were waited for; matrix products, arithmetic and copies ran while one was open for 13% of the time, Pallas kernels for 0%

profile of v1, /device:TPU:0, one launch (start us, length us, event | category | flops | bytes accessed | tf_op | source)
XLA Modules:
  0.0 1492.1 jit_solution(10714820369222798011)
XLA Ops:
  16.6 34.9 %all-gather.17.cloned.1.call-done = bf16[1024,2048]{1,0:T(8,128)(2,1)} async-done(((bf16[128,2048]{1,0:T(8,128)(2,1)}), bf16[1024,2048]{1,0:T(8,128)(2,1)}) %all-gather.17.cloned.1.call-update) | async-done | bytes 4194320 | tf_op jit(solution)/shard_map/all_gather | solution.py:227
  51.5 4.5 convolution_convert_fusion.4
  63.0 4.7 fusion.168
  68.3 22.4 %all-gather.13.cloned.1.call-done = bf16[1024,2048]{1,0:T(8,128)(2,1)} async-done(((bf16[128,2048]{1,0:T(8,128)(2,1)}), bf16[1024,2048]{1,0:T(8,128)(2,1)}) %all-gather.13.cloned.1.call-update) | async-done | bytes 4194320 | tf_op jit(solution)/shard_map/all_gather | solution.py:227
  90.8 4.5 convolution_convert_fusion.5
  102.2 5.7 fusion.166
  108.0 58.2 %reduce-scatter.13.cloned.1.call-done = f32[128,2048]{1,0:T(8,128)} async-done(((f32[1024,2048]{1,0:T(8,128)}), f32[128,2048]{1,0:T(8,128)}) %reduce-scatter.13.cloned.1.call-update) | async-done | bytes 1048592 | tf_op jit(solution)/shard_map/reduce_scatter | solution.py:242
  166.2 75.6 %reduce-scatter.9.cloned.1.call-done = f32[128,2048]{1,0:T(8,128)} async-done(((f32[1024,2048]{1,0:T(8,128)}), f32[128,2048]{1,0:T(8,128)}) %reduce-scatter.9.cloned.1.call-update) | async-done | bytes 1048592 | tf_op jit(solution)/shard_map/reduce_scatter | solution.py:242
  241.8 2.8 multiply_reduce_fusion.9
  248.0 4.8 constant_dynamic-update-slice_fusion.4
  255.2 27.2 %all-gather.15.cloned.1.call-done = bf16[1024,2048]{1,0:T(8,128)(2,1)} async-done(((bf16[128,2048]{1,0:T(8,128)(2,1)}), bf16[1024,2048]{1,0:T(8,128)(2,1)}) %all-gather.15.cloned.1.call-update) | async-done | bytes 4194320 | tf_op jit(solution)/shard_map/all_gather | solution.py:251
  282.4 15.0 %fusion.167 = f32[1024,2048]{1,0:T(8,128)} fusion(bf16[1024,2048]{1,0:T(8,128)(2,1)} %all-gather.15.cloned.1.call-done, bf16[2048,2048]{1,0:T(8,128)(2,1)} %constant_dynamic-update-slice_fusion.3), kind=kOutput, calls=%fused_computation.320 | convolution fusion | flops 8589934592 | bytes 20971520 | tf_op jit(solution)/shard_map/dot_general | solution.py:252
  297.4 24.1 %all-gather.25.cloned.1.call-done = bf16[1,1,1024,2048]{3,2,1,0:T(8,128)(2,1)} async-done(((bf16[1,1,128,2048]{3,2,1,0:T(8,128)(2,1)}), bf16[1,1,1024,2048]{3,2,1,0:T(8,128)(2,1)}) %all-gather.25.cloned.1.call-update) | async-done | bytes 4194320 | tf_op jit(solution)/shard_map/all_gather | solution.py:265
  321.5 13.2 multiply_convert_fusion.3
  336.8 13.3 fusion.12
  350.1 71.3 %reduce-scatter.17.cloned.1.call-done = f32[128,2048]{1,0:T(8,128)} async-done(((f32[1024,2048]{1,0:T(8,128)}), f32[128,2048]{1,0:T(8,128)}) %reduce-scatter.17.cloned.1.call-update) | async-done | bytes 1048592 | tf_op jit(solution)/shard_map/reduce_scatter | solution.py:272
  421.5 3.0 multiply_reduce_fusion.1
  425.3 36.1 %all-gather.19.cloned.1.call-done = bf16[1024,2048]{1,0:T(8,128)(2,1)} async-done(((bf16[128,2048]{1,0:T(8,128)(2,1)}), bf16[1024,2048]{1,0:T(8,128)(2,1)}) %all-gather.19.cloned.1.call-update) | async-done | bytes 4194320 | tf_op jit(solution)/shard_map/all_gather | solution.py:251
  461.4 14.6 fusion.169
  476.0 24.7 %all-gather.27.cloned.1.call-done = bf16[1,1,1024,2048]{3,2,1,0:T(8,128)(2,1)} async-done(((bf16[1,1,128,2048]{3,2,1,0:T(8,128)(2,1)}), bf16[1,1,1024,2048]{3,2,1,0:T(8,128)(2,1)}) %all-gather.27.cloned.1.call-update) | async-done | bytes 4194320 | tf_op jit(solution)/shard_map/all_gather | solution.py:265
  500.7 13.2 multiply_convert_fusion.1
  516.0 13.3 fusion.10
  529.7 9.7 convolution_convert_fusion.3
  539.5 10.4 convolution_convert_fusion.2
  550.0 50.7 %reduce-scatter.21.cloned.1.call-done = f32[128,2048]{1,0:T(8,128)} async-done(((f32[1024,2048]{1,0:T(8,128)}), f32[128,2048]{1,0:T(8,128)}) %reduce-scatter.21.cloned.1.call-update) | async-done | bytes 1048592 | tf_op jit(solution)/shard_map/reduce_scatter | solution.py:272
  602.2 53.8 %reduce-scatter.11.cloned.1.call-done = bf16[128,2048]{1,0:T(8,128)(2,1)} async-done(((bf16[1024,2048]{1,0:T(8,128)(2,1)}), bf16[128,2048]{1,0:T(8,128)(2,1)}) %reduce-scatter.11.cloned.1.call-update) | async-done | bytes 524304 | tf_op jit(solution)/shard_map/reduce_scatter | solution.py:257
  656.0 55.5 %reduce-scatter.15.cloned.1.call-done = bf16[128,2048]{1,0:T(8,128)(2,1)} async-done(((bf16[1024,2048]{1,0:T(8,128)(2,1)}), bf16[128,2048]{1,0:T(8,128)(2,1)}) %reduce-scatter.15.cloned.1.call-update) | async-done | bytes 524304 | tf_op jit(solution)/shard_map/reduce_scatter | solution.py:257
  711.5 4.6 fusion.153
  716.8 36.1 %all-gather.23.cloned.1.call-done = bf16[1024,2048]{1,0:T(8,128)(2,1)} async-done(((bf16[128,2048]{1,0:T(8,128)(2,1)}), bf16[1024,2048]{1,0:T(8,128)(2,1)}) %all-gather.23.cloned.1.call-update) | async-done | bytes 4194320 | tf_op jit(solution)/shard_map/all_gather | solution.py:278
  753.0 4.6 fusion.65
  763.3 5.9 convolution_convert_fusion
  769.5 22.5 %all-gather.21.cloned.1.call-done = bf16[1024,2048]{1,0:T(8,128)(2,1)} async-done(((bf16[128,2048]{1,0:T(8,128)(2,1)}), bf16[1024,2048]{1,0:T(8,128)(2,1)}) %all-gather.21.cloned.1.call-update) | async-done | bytes 4194320 | tf_op jit(solution)/shard_map/all_gather | solution.py:278
  792.0 4.6 fusion.61
  802.3 6.0 convolution_convert_fusion.1
  809.2 4.8 fusion.72
  814.1 3.6 add_convert_fusion.2
  818.0 15.8 %fusion.11 = f32[2048,2048]{1,0:T(8,128)} fusion(bf16[1024,2048]{1,0:T(8,128)(2,1)} %all-gather.15.cloned.1.call-done, bf16[1024,1024]{1,0:T(8,128)(2,1)} %copy-done.109, bf16[1024,1024]{1,0:T(8,128)(2,1)} %copy-done.108), kind=kOutput, calls=%fused_computation.26 | convolution fusion | flops 8598323200 | bytes 25165824 | tf_op jit(solution)/shard_map/dot_general | solution.py:27
  833.9 4.6 fusion
  838.5 6.2 add_convert_fusion.1
  844.6 16.8 %add_convert_fusion = bf16[2048,2048]{1,0:T(8,128)(2,1)} fusion(f32[2048,2048]{1,0:T(8,128)} %fusion.11, bf16[1024,2048]{1,0:T(8,128)(2,1)} %all-gather.19.cloned.1.call-done, bf16[1024,1024]{1,0:T(8,128)(2,1)} %copy-done.112, bf16[1024,1024]{1,0:T(8,128)(2,1)S(1)} %copy-done.111), kind=kOutput, calls=%fused_computation | convolution fusion | flops 8606711808 | bytes 33554432 | tf_op jit(solution)/shard_map/dot_general | solution.py:27
  870.1 13.1 psum.47
  883.9 18.8 %reduce-scatter.19.cloned.1.call-done = bf16[128,2048]{1,0:T(8,128)(2,1)} async-done(((bf16[1024,2048]{1,0:T(8,128)(2,1)}), bf16[128,2048]{1,0:T(8,128)(2,1)}) %reduce-scatter.19.cloned.1.call-update) | async-done | bytes 524304 | tf_op jit(solution)/shard_map/reduce_scatter | solution.py:306
  904.6 48.5 %all-reduce.6 = (f32[2048]{0:T(1024)}, f32[2048]{0:T(1024)}) all-reduce(f32[2048]{0:T(1024)S(1)} %add.350, f32[2048]{0:T(1024)S(1)} %add.351), channel_id=1, replica_groups=mesh['heads'=8,'batch'=4] {'heads','batch'}, use_global_device_ids=true, to_apply=%region_42.43 | all-reduce | flops 4096 | bytes 32768 | tf_op jit(solution)/shard_map/psum | solution.py:319
  956.9 63.6 %all-gather.29.cloned.1.call-done = bf16[8192,384]{1,0:T(8,128)(2,1)} async-done(((bf16[2048,384]{1,0:T(8,128)(2,1)}), bf16[8192,384]{1,0:T(8,128)(2,1)}) %all-gather.29.cloned.1.call-update) | async-done | bytes 6291472 | tf_op jit(solution)/shard_map/all_gather | solution.py:17
  1020.5 4.7 reduce_sum.294
  1027.0 439.4 %all-reduce.10.cloned.1.call-done = (bf16[2048,2048]{1,0:T(8,128)(2,1)}, bf16[128,2048]{1,0:T(8,128)(2,1)}, bf16[1024,2048]{1,0:T(8,128)(2,1)}) async-done(((bf16[2048,2048]{1,0:T(8,128)(2,1)}, bf16[128,2048]{1,0:T(8,128)(2,1)}, bf16[1024,2048]{1,0:T(8,128)(2,1)}), (bf16[2048,2048]{1,0:T(8,128)(2,1)}, bf16[128,2048]{1,0:T(8,128)(2,1)}, bf16[1024,2048]{1,0:T(8,128)(2,1)})) %all-reduce.10.cloned.1.call-update) | async-done | bytes 13107216 | tf_op jit(solution)/shard_map/psum | solution.py:315
  1466.5 11.9 fusion.155
  1478.4 4.4 convert_element_type.298
  (371 shorter events, 64.2 us)
Async XLA Ops:
  7.2 55.8 %copy-start = (bf16[128,2048]{1,0:T(8,128)(2,1)S(1)}, bf16[128,2048]{1,0:T(8,128)(2,1)}, u32[]{:S(2)}) copy-start(bf16[128,2048]{1,0:T(8,128)(2,1)} %param.57) | copy-start | bytes 1572868
  7.2 44.3 %all-gather.17.cloned.1.call-start = ((), (), s32[]{:S(2)}) async-start(), calls=%async_computation.12 | async-start | bytes 4718592 | tf_op jit(solution)/shard_map/all_gather | solution.py:227
  12.0 78.8 %all-gather.13.cloned.1.call-start = ((), (), s32[]{:S(2)}) async-start(), calls=%async_computation.8 | async-start | bytes 4718592 | tf_op jit(solution)/shard_map/all_gather | solution.py:227
  12.7 153.4 %reduce-scatter.13.cloned.1.call-start = ((), (), s32[]{:S(2)}) async-start(), calls=%async_computation.13 | async-start | bytes 9437184 | tf_op jit(solution)/shard_map/reduce_scatter | solution.py:242
  13.8 44.4 %copy-start.97 = (pred[512]{0:T(512)(128)(4,1)}, pred[512]{0:T(512)(128)(4,1)S(1)}, u32[]{:S(2)}) copy-start(pred[512]{0:T(512)(128)(4,1)S(1)} %get-tuple-element.267) | copy-start | bytes 1540
  13.9 44.3 %copy-start.90 = (s32[512]{0:T(512)}, s32[512]{0:T(512)S(1)}, u32[]{:S(2)}) copy-start(s32[512]{0:T(512)S(1)} %get-tuple-element.329) | copy-start | bytes 6148
  13.9 44.3 %copy-start.92 = (s32[512]{0:T(512)}, s32[512]{0:T(512)S(1)}, u32[]{:S(2)}) copy-start(s32[512]{0:T(512)S(1)} %get-tuple-element.330) | copy-start | bytes 6148
  67.7 174.1 %reduce-scatter.9.cloned.1.call-start = ((), (), s32[]{:S(2)}) async-start(), calls=%async_computation.9 | async-start | bytes 9437184 | tf_op jit(solution)/shard_map/reduce_scatter | solution.py:242
  68.2 29.2 %copy-start.95 = (pred[512]{0:T(512)(128)(4,1)}, pred[512]{0:T(512)(128)(4,1)S(1)}, u32[]{:S(2)}) copy-start(pred[512]{0:T(512)(128)(4,1)S(1)} %get-tuple-element.265) | copy-start | bytes 1540
  68.3 29.1 %copy-start.86 = (s32[512]{0:T(512)}, s32[512]{0:T(512)S(1)}, u32[]{:S(2)}) copy-start(s32[512]{0:T(512)S(1)} %get-tuple-element.327) | copy-start | bytes 6148
  68.3 29.1 %copy-start.88 = (s32[512]{0:T(512)}, s32[512]{0:T(512)S(1)}, u32[]{:S(2)}) copy-start(s32[512]{0:T(512)S(1)} %get-tuple-element.328) | copy-start | bytes 6148
  107.9 133.9 %copy-start.9 = (bf16[2,1,128,2048]{3,2,1,0:T(8,128)(2,1)S(1)}, bf16[2,1,128,2048]{3,2,1,0:T(8,128)(2,1)}, u32[]{:S(2)}) copy-start(bf16[2,1,128,2048]{3,2,1,0:T(8,128)(2,1)} %param.50) | copy-start | bytes 3145732
  108.0 136.6 %copy-start.62 = (f32[2048]{0:T(1024)S(1)}, f32[2048]{0:T(1024)}, u32[]{:S(2)}) copy-start(f32[2048]{0:T(1024)} %param.62) | copy-start | bytes 24580
  108.0 174.4 %all-gather.15.cloned.1.call-start = ((), (), s32[]{:S(2)}) async-start(), calls=%async_computation.10 | async-start | bytes 4718592 | tf_op jit(solution)/shard_map/all_gather | solution.py:251
  245.6 75.9 %all-gather.25.cloned.1.call-start = ((), (), s32[]{:S(2)}) async-start(), calls=%async_computation.22 | async-start | bytes 4718592 | tf_op jit(solution)/shard_map/all_gather | solution.py:265
  247.9 173.6 %reduce-scatter.17.cloned.1.call-start = ((), (), s32[]{:S(2)}) async-start(), calls=%async_computation.16 | async-start | bytes 9437184 | tf_op jit(solution)/shard_map/reduce_scatter | solution.py:272
  350.1 71.4 %copy-start.11 = (f32[128,2048]{1,0:T(8,128)S(1)}, f32[128,2048]{1,0:T(8,128)}, u32[]{:S(2)}) copy-start(f32[128,2048]{1,0:T(8,128)} %get-tuple-element.303) | copy-start | bytes 3145732
  350.1 111.3 %all-gather.19.cloned.1.call-start = ((), (), s32[]{:S(2)}) async-start(), calls=%async_computation.14 | async-start | bytes 4718592 | tf_op jit(solution)/shard_map/all_gather | solution.py:251
  424.5 76.2 %all-gather.27.cloned.1.call-start = ((), (), s32[]{:S(2)}) async-start(), calls=%async_computation.23 | async-start | bytes 4718592 | tf_op jit(solution)/shard_map/all_gather | solution.py:265
  425.2 175.5 %reduce-scatter.21.cloned.1.call-start = ((), (), s32[]{:S(2)}) async-start(), calls=%async_computation.19 | async-start | bytes 9437184 | tf_op jit(solution)/shard_map/reduce_scatter | solution.py:272
  529.3 126.7 %reduce-scatter.11.cloned.1.call-start = ((), (), s32[]{:S(2)}) async-start(), calls=%async_computation.11 | async-start | bytes 4718592 | tf_op jit(solution)/shard_map/reduce_scatter | solution.py:257
  539.5 172.0 %reduce-scatter.15.cloned.1.call-start = ((), (), s32[]{:S(2)}) async-start(), calls=%async_computation.15 | async-start | bytes 4718592 | tf_op jit(solution)/shard_map/reduce_scatter | solution.py:257
  550.0 203.0 %all-gather.23.cloned.1.call-start = ((), (), s32[]{:S(2)}) async-start(), calls=%async_computation.20 | async-start | bytes 4718592 | tf_op jit(solution)/shard_map/all_gather | solution.py:278
  716.1 41.5 %copy-start.6 = (f32[512,512]{0,1:T(8,128)S(1)}, f32[512,512]{0,1:T(8,128)}, u32[]{:S(2)}) copy-start(f32[512,512]{0,1:T(8,128)} %copy-done.5) | copy-start | bytes 3145732
  716.1 41.5 %copy-start.67 = (f32[512]{0:T(512)S(1)}, f32[512]{0:T(512)}, u32[]{:S(2)}) copy-start(f32[512]{0:T(512)} %copy-done.66) | copy-start | bytes 6148
  716.1 75.9 %all-gather.21.cloned.1.call-start = ((), (), s32[]{:S(2)}) async-start(), calls=%async_computation.17 | async-start | bytes 4718592 | tf_op jit(solution)/shard_map/all_gather | solution.py:278
  716.7 41.2 %copy-start.8 = (f32[512,512]{0,1:T(8,128)S(1)}, f32[512,512]{0,1:T(8,128)}, u32[]{:S(2)}) copy-start(f32[512,512]{0,1:T(8,128)} %copy-done.7) | copy-start | bytes 3145732
  716.7 41.2 %copy-start.71 = (f32[512]{0:T(512)S(1)}, f32[512]{0:T(512)}, u32[]{:S(2)}) copy-start(f32[512]{0:T(512)} %copy-done.70) | copy-start | bytes 6148
  716.7 41.6 %copy-start.76 = (f32[512]{0:T(512)S(1)}, f32[512]{0:T(512)}, u32[]{:S(2)}) copy-start(f32[512]{0:T(512)} %copy-done.75) | copy-start | bytes 6148
  716.7 41.6 %copy-start.15 = (bf16[1024,384]{0,1:T(8,128)(2,1)S(1)}, bf16[1024,384]{0,1:T(8,128)(2,1)}, u32[]{:S(2)}) copy-start(bf16[1024,384]{0,1:T(8,128)(2,1)} %copy-done.14) | copy-start | bytes 2359300
  716.7 41.6 %copy-start.85 = (f32[512]{0:T(512)S(1)}, f32[512]{0:T(512)}, u32[]{:S(2)}) copy-start(f32[512]{0:T(512)} %copy-done.84) | copy-start | bytes 6148
  716.7 41.6 %copy-start.91 = (s32[512]{0:T(512)S(1)}, s32[512]{0:T(512)}, u32[]{:S(2)}) copy-start(s32[512]{0:T(512)} %copy-done.90) | copy-start | bytes 6148
  716.8 41.6 %copy-start.93 = (s32[512]{0:T(512)S(1)}, s32[512]{0:T(512)}, u32[]{:S(2)}) copy-start(s32[512]{0:T(512)} %copy-done.92) | copy-start | bytes 6148
  716.8 41.6 %copy-start.98 = (pred[512]{0:T(512)(128)(4,1)S(1)}, pred[512]{0:T(512)(128)(4,1)}, u32[]{:S(2)}) copy-start(pred[512]{0:T(512)(128)(4,1)} %copy-done.97) | copy-start | bytes 1540
  716.8 167.1 %reduce-scatter.23.cloned.1.call-start = ((), (), s32[]{:S(2)}) async-start(), calls=%async_computation.21 | async-start | bytes 4718592 | tf_op jit(solution)/shard_map/reduce_scatter | solution.py:306
  769.3 28.2 %copy-start.13 = (bf16[1024,384]{0,1:T(8,128)(2,1)S(1)}, bf16[1024,384]{0,1:T(8,128)(2,1)}, u32[]{:S(2)}) copy-start(bf16[1024,384]{0,1:T(8,128)(2,1)} %copy-done.12) | copy-start | bytes 2359300
  769.3 28.2 %copy-start.83 = (f32[512]{0:T(512)S(1)}, f32[512]{0:T(512)}, u32[]{:S(2)}) copy-start(f32[512]{0:T(512)} %copy-done.82) | copy-start | bytes 6148
  769.3 28.2 %copy-start.87 = (s32[512]{0:T(512)S(1)}, s32[512]{0:T(512)}, u32[]{:S(2)}) copy-start(s32[512]{0:T(512)} %copy-done.86) | copy-start | bytes 6148
  769.3 28.2 %copy-start.89 = (s32[512]{0:T(512)S(1)}, s32[512]{0:T(512)}, u32[]{:S(2)}) copy-start(s32[512]{0:T(512)} %copy-done.88) | copy-start | bytes 6148
  769.3 28.2 %copy-start.96 = (pred[512]{0:T(512)(128)(4,1)S(1)}, pred[512]{0:T(512)(128)(4,1)}, u32[]{:S(2)}) copy-start(pred[512]{0:T(512)(128)(4,1)} %copy-done.95) | copy-start | bytes 1540
  769.3 133.4 %reduce-scatter.19.cloned.1.call-start = ((), (), s32[]{:S(2)}) async-start(), calls=%async_computation.18 | async-start | bytes 4718592 | tf_op jit(solution)/shard_map/reduce_scatter | solution.py:306
  808.3 212.2 %all-gather.29.cloned.1.call-start = ((), (), s32[]{:S(2)}) async-start(), calls=%async_computation.24 | async-start | bytes 7864320 | tf_op jit(solution)/shard_map/all_gather | solution.py:17
  817.7 648.7 %all-reduce.10.cloned.1.call-start = ((), (), s32[]{:S(2)}) async-start(), calls=%async_computation.25 | async-start | bytes 26214400 | tf_op jit(solution)/shard_map/psum | solution.py:315
  865.7 37.0 %copy-start.10 = (bf16[2,1,128,2048]{3,2,1,0:T(8,128)(2,1)S(1)}, bf16[2,1,128,2048]{3,2,1,0:T(8,128)(2,1)}, u32[]{:S(2)}) copy-start(bf16[2,1,128,2048]{3,2,1,0:T(8,128)(2,1)} %param.50) | copy-start | bytes 3145732
  865.7 37.0 %copy-start.63 = (f32[2048]{0:T(1024)S(1)}, f32[2048]{0:T(1024)}, u32[]{:S(2)}) copy-start(f32[2048]{0:T(1024)} %param.61) | copy-start | bytes 24580
  865.7 37.0 %copy-start.79 = (f32[128]{0:T(128)S(1)}, f32[128]{0:T(128)}, u32[]{:S(2)}) copy-start(f32[128]{0:T(128)} %copy-done.78) | copy-start | bytes 1540
  865.7 37.0 %copy-start.81 = (f32[128]{0:T(128)S(1)}, f32[128]{0:T(128)}, u32[]{:S(2)}) copy-start(f32[128]{0:T(128)} %copy-done.80) | copy-start | bytes 1540
  865.7 87.4 %copy-start.20 = (f32[128,2048]{1,0:T(8,128)S(1)}, f32[128,2048]{1,0:T(8,128)}, u32[]{:S(2)}) copy-start(f32[128,2048]{1,0:T(8,128)} %get-tuple-element.274) | copy-start | bytes 3145732
  (83 other events, 423.7 us)
Sparse Core Ops, SparseCore 0:
  12.1 39.4 all-gather.16
  54.0 36.7 all-gather.12
  94.8 71.3 reduce-scatter.12
  170.5 71.2 reduce-scatter.8
  245.7 36.6 all-gather.14
  284.7 36.7 all-gather.24
  350.2 71.2 reduce-scatter.16
  424.6 36.6 all-gather.18
  464.0 36.7 all-gather.26
  529.4 71.2 reduce-scatter.20
  604.6 51.3 reduce-scatter.10
  660.2 51.3 reduce-scatter.14
  716.2 36.6 all-gather.22
  755.3 36.7 all-gather.20
  795.8 51.3 reduce-scatter.22
  851.3 51.3 reduce-scatter.18
  904.1 116.3 all-gather.28
  1023.8 442.6 all-reduce.9
